TPU v7x, 32 devices: a whole 2x2x4 slice. The times are simulated.
32 devices in a mesh: dp: 8 (over y, x, core), tp: 4 (over z).
Axes of the slice: x: 2, y: 2, z: 4, core: 2. Of those that a mesh axis runs over, the one named last changes fastest.
Arguments:
- tokens: bfloat16 [20480, 768], P(('dp', 'tp')), may hold values from -6 to 6
- w_query: bfloat16 [768, 768], P('dp', 'tp'), may hold values from -0.3125 to 0.3125
- w_key: bfloat16 [768, 768], P('dp', 'tp'), may hold values from -0.3125 to 0.3125
- w_value: bfloat16 [768, 768], P('dp', 'tp'), may hold values from -0.21875 to 0.21875
- b_query: bfloat16 [768], P('dp'), may hold values from -3 to 3
- b_value: bfloat16 [768], P('dp'), may hold values from -3 to 3
- w_out: bfloat16 [768, 768], P('dp', 'tp'), may hold values from -0.875 to 0.875
- b_out: bfloat16 [768], P('dp'), may hold values from -3 to 3
- gain_attn: bfloat16 [768], P('dp'), may hold values from 0.25 to 1.75
- shift_attn: bfloat16 [768], P('dp'), may hold values from -3 to 3
- w_up: bfloat16 [768, 3072], P('dp', 'tp'), may hold values from -0.21875 to 0.21875
- b_up: bfloat16 [3072], P('dp'), may hold values from -3 to 3
- w_down: bfloat16 [768, 3072], P('dp', 'tp'), may hold values from -0.15625 to 0.15625
- b_down: bfloat16 [768], P('dp'), may hold values from -3 to 3
- gain_ffn: bfloat16 [768], P('dp'), may hold values from 0.25 to 1.75
- shift_ffn: bfloat16 [768], P('dp'), may hold values from -3 to 3
- lengths: int32 [16], replicated, may hold values from 1024 to 1536, as said below
- deal_order: int32 [16], replicated, may hold values from 0 to 15, as said below
- cotangent: bfloat16 [20480, 768], P(('dp', 'tp')), may hold values from -6 to 6
Outputs:
- encoder_output: bfloat16 [20480, 768], P(('dp', 'tp'))
- grad_tokens: float32 [20480, 768], P(('dp', 'tp'))
- grad_w_query: float32 [768, 768], P('dp', 'tp')
- grad_w_key: float32 [768, 768], P('dp', 'tp')
- grad_w_value: float32 [768, 768], P('dp', 'tp')
- grad_b_query: float32 [768], P('dp')
- grad_b_value: float32 [768], P('dp')
- grad_w_out: float32 [768, 768], P('dp', 'tp')
- grad_b_out: float32 [768], P('dp')
- grad_gain_attn: float32 [768], P('dp')
- grad_shift_attn: float32 [768], P('dp')
- grad_w_up: float32 [768, 3072], P('dp', 'tp')
- grad_b_up: float32 [3072], P('dp')
- grad_w_down: float32 [768, 3072], P('dp', 'tp')
- grad_b_down: float32 [768], P('dp')
- grad_gain_ffn: float32 [768], P('dp')
- grad_shift_ffn: float32 [768], P('dp')
Inputs may be any that keep to these rules, and one draw needn't show every extreme that they name: Group g holds sequence deal_order[2 g] in slot 0 and deal_order[2 g + 1] in slot 1; the two lengths of a group add up to 2560, and each is at least 1024. `deal_order`: each of 0 to 15 appears once.
All inputs are finite; a program needn't handle non-finite values.
Results may differ from a plain program's by a relative error of at most 0.015.
The roundings to bfloat16 on the way count: a program that leaves them out, or rounds other values in their place, can miss the bound.
Values may be sent and summed in bfloat16 or wider, within the bound.
A program may use at most 128 MiB of HBM per device.

v0:
```python
import jax
import jax.numpy as jnp
from jax import lax
from jax.sharding import PartitionSpec as P

HD = 64
EPS = 1e-05
SQRT_HALF = 0.7071067811865476
INV_ROOT_TAU = 0.3989422804014327


def normalize_layer(resid):
    center = resid - jnp.mean(resid, axis=-1, keepdims=True)
    inverse_deviation = lax.rsqrt(jnp.mean(center * center, axis=-1, keepdims=True) + EPS)
    return (center * inverse_deviation, inverse_deviation)


def normalize_backward(output_gradient, centered_scaled, inverse_deviation, norm_gain):
    scaled_rows = output_gradient * norm_gain
    return inverse_deviation * (
        scaled_rows
        - jnp.mean(scaled_rows, axis=-1, keepdims=True)
        - centered_scaled * jnp.mean(scaled_rows * centered_scaled, axis=-1, keepdims=True)
    )


def gelu_slope(pre_act):
    return (
        0.5 * (1.0 + lax.erf(pre_act * SQRT_HALF))
        + pre_act * jnp.exp(-0.5 * pre_act * pre_act) * INV_ROOT_TAU
    )


def contract_last(left, right):
    return lax.dot_general(
        left, right, (((1,), (1,)), ((), ())), preferred_element_type=jnp.float32
    )


def contract_first(left, right):
    return lax.dot_general(
        left, right, (((0,), (0,)), ((), ())), preferred_element_type=jnp.float32
    )


def body(
    tokens,
    w_query,
    w_key,
    w_value,
    b_query,
    b_value,
    w_out,
    b_out,
    gain_attn,
    shift_attn,
    w_up,
    b_up,
    w_down,
    b_down,
    gain_ffn,
    shift_ffn,
    lengths,
    deal_order,
    cotangent,
):
    own_rows = tokens.shape[0]
    tp_index = lax.axis_index("tp")
    group_rows = own_rows * lax.axis_size("tp")
    params = (
        w_query,
        w_key,
        w_value,
        w_out,
        w_up,
        w_down,
        b_query,
        b_value,
        b_out,
        gain_attn,
        shift_attn,
        b_up,
        b_down,
        gain_ffn,
        shift_ffn,
    )
    gathered = (
        lax.all_gather(params[0], "dp", axis=0, tiled=True),
        lax.all_gather(params[1], "dp", axis=0, tiled=True),
        lax.all_gather(params[2], "dp", axis=0, tiled=True),
        lax.all_gather(params[3], "dp", axis=0, tiled=True),
        lax.all_gather(params[4], "dp", axis=0, tiled=True),
        lax.all_gather(params[5], "dp", axis=0, tiled=True),
        lax.all_gather(params[6], "dp", axis=0, tiled=True),
        lax.all_gather(params[7], "dp", axis=0, tiled=True),
        lax.all_gather(params[8], "dp", axis=0, tiled=True),
        lax.all_gather(params[9], "dp", axis=0, tiled=True),
        lax.all_gather(params[10], "dp", axis=0, tiled=True),
        lax.all_gather(params[11], "dp", axis=0, tiled=True),
        lax.all_gather(params[12], "dp", axis=0, tiled=True),
        lax.all_gather(params[13], "dp", axis=0, tiled=True),
        lax.all_gather(params[14], "dp", axis=0, tiled=True),
    )
    (
        query_weight,
        key_weight,
        value_weight,
        out_weight,
        up_weight,
        down_weight,
        query_bias,
        value_bias,
        out_bias,
        first_norm_gain,
        first_norm_shift,
        up_bias,
        down_projection_bias,
        second_norm_gain,
        second_norm_shift,
    ) = gathered
    width = query_weight.shape[1]
    hidden_width = up_weight.shape[1]
    heads = width // HD
    block = min(512, group_rows)
    blocks = group_rows // block
    scale = HD ** (-0.5)
    pair = lax.dynamic_slice_in_dim(deal_order, 2 * lax.axis_index("dp"), 2)
    first_len = jnp.sum(
        jnp.where(jnp.arange(lengths.shape[0], dtype=jnp.int32) == pair[0], lengths, 0)
    )
    segment = (jnp.arange(group_rows, dtype=jnp.int32) >= first_len).astype(jnp.int32)
    own_query_bias = lax.dynamic_slice_in_dim(query_bias, tp_index * width, width).astype(
        jnp.float32
    )
    own_value_bias = lax.dynamic_slice_in_dim(value_bias, tp_index * width, width).astype(
        jnp.float32
    )
    own_up_bias = lax.dynamic_slice_in_dim(up_bias, tp_index * hidden_width, hidden_width).astype(
        jnp.float32
    )
    input_full = lax.all_gather(tokens, "tp", axis=0, tiled=True)
    query_rows = (
        jnp.dot(input_full, query_weight, preferred_element_type=jnp.float32) + own_query_bias
    ).astype(jnp.bfloat16)
    key_rows = jnp.dot(input_full, key_weight, preferred_element_type=jnp.float32).astype(
        jnp.bfloat16
    )
    value_rows = (
        jnp.dot(input_full, value_weight, preferred_element_type=jnp.float32) + own_value_bias
    ).astype(jnp.bfloat16)
    key_heads = key_rows.reshape(group_rows, heads, HD)
    value_heads = value_rows.reshape(group_rows, heads, HD)
    query_blocks = query_rows.reshape(blocks, block, heads, HD)
    seg_blocks = segment.reshape(blocks, block)

    def masked_scores(query_block, seg_block):
        scores = (
            jnp.einsum("qhd,khd->hqk", query_block, key_heads, preferred_element_type=jnp.float32)
            * scale
        )
        allowed = seg_block[:, None] == segment[None, :]
        return jnp.where(allowed[None], scores, -1e30)

    def attend(inputs):
        query_block, seg_block = inputs
        scores = masked_scores(query_block, seg_block)
        highest = jnp.max(scores, axis=-1, keepdims=True)
        raised = jnp.exp(scores - highest)
        total = jnp.sum(raised, axis=-1, keepdims=True)
        shares = (raised / total).astype(jnp.bfloat16)
        mixed = jnp.einsum("hqk,khd->qhd", shares, value_heads, preferred_element_type=jnp.float32)
        return (
            mixed.astype(jnp.bfloat16).reshape(block, width),
            (highest + jnp.log(total))[:, :, 0],
        )

    mixed_blocks, log_totals = lax.map(attend, (query_blocks, seg_blocks))
    mixed_rows = mixed_blocks.reshape(group_rows, width)
    attn_term = lax.psum_scatter(
        contract_last(mixed_rows, out_weight), "tp", scatter_dimension=0, tiled=True
    )
    first_residual = tokens.astype(jnp.float32) + attn_term + out_bias.astype(jnp.float32)
    first_centered_scaled, first_inverse_deviation = normalize_layer(first_residual)
    normalized_rows = first_centered_scaled * first_norm_gain.astype(
        jnp.float32
    ) + first_norm_shift.astype(jnp.float32)
    normed_full = lax.all_gather(normalized_rows.astype(jnp.bfloat16), "tp", axis=0, tiled=True)
    pre_act = jnp.dot(normed_full, up_weight, preferred_element_type=jnp.float32) + own_up_bias
    hidden = jax.nn.gelu(pre_act, approximate=False).astype(jnp.bfloat16)
    feedforward_term = lax.psum_scatter(
        contract_last(hidden, down_weight), "tp", scatter_dimension=0, tiled=True
    )
    second_centered_scaled, second_inverse_deviation = normalize_layer(
        normalized_rows + feedforward_term + down_projection_bias.astype(jnp.float32)
    )
    encoder_output = (
        second_centered_scaled * second_norm_gain.astype(jnp.float32)
        + second_norm_shift.astype(jnp.float32)
    ).astype(jnp.bfloat16)
    gathered = (
        lax.all_gather(params[0], "dp", axis=0, tiled=True),
        lax.all_gather(params[1], "dp", axis=0, tiled=True),
        lax.all_gather(params[2], "dp", axis=0, tiled=True),
        lax.all_gather(params[3], "dp", axis=0, tiled=True),
        lax.all_gather(params[4], "dp", axis=0, tiled=True),
        lax.all_gather(params[5], "dp", axis=0, tiled=True),
        lax.all_gather(params[6], "dp", axis=0, tiled=True),
        lax.all_gather(params[7], "dp", axis=0, tiled=True),
        lax.all_gather(params[8], "dp", axis=0, tiled=True),
        lax.all_gather(params[9], "dp", axis=0, tiled=True),
        lax.all_gather(params[10], "dp", axis=0, tiled=True),
        lax.all_gather(params[11], "dp", axis=0, tiled=True),
        lax.all_gather(params[12], "dp", axis=0, tiled=True),
        lax.all_gather(params[13], "dp", axis=0, tiled=True),
        lax.all_gather(params[14], "dp", axis=0, tiled=True),
    )
    (
        query_weight,
        key_weight,
        value_weight,
        out_weight,
        up_weight,
        down_weight,
        query_bias,
        value_bias,
        out_bias,
        first_norm_gain,
        first_norm_shift,
        up_bias,
        down_projection_bias,
        second_norm_gain,
        second_norm_shift,
    ) = gathered
    output_gradient = cotangent.astype(jnp.float32)
    second_gain_gradient = jnp.sum(output_gradient * second_centered_scaled, axis=0)
    grad_shift_two = jnp.sum(output_gradient, axis=0)
    second_residual_gradient = normalize_backward(
        output_gradient,
        second_centered_scaled,
        second_inverse_deviation,
        second_norm_gain.astype(jnp.float32),
    )
    grad_ffn_full = lax.all_gather(
        second_residual_gradient.astype(jnp.bfloat16), "tp", axis=0, tiled=True
    )
    grad_down_bias = jnp.sum(grad_ffn_full, axis=0, dtype=jnp.float32)
    grad_down_weight = contract_first(grad_ffn_full, hidden)
    grad_hidden = jnp.dot(grad_ffn_full, down_weight, preferred_element_type=jnp.float32)
    grad_pre = (grad_hidden * gelu_slope(pre_act)).astype(jnp.bfloat16)
    grad_up_bias = jnp.sum(grad_pre, axis=0, dtype=jnp.float32)
    grad_up_weight = contract_first(normed_full, grad_pre)
    normalized_gradient = second_residual_gradient + lax.psum_scatter(
        contract_last(grad_pre, up_weight), "tp", scatter_dimension=0, tiled=True
    )
    first_gain_gradient = jnp.sum(normalized_gradient * first_centered_scaled, axis=0)
    grad_shift_one = jnp.sum(normalized_gradient, axis=0)
    first_residual_gradient = normalize_backward(
        normalized_gradient,
        first_centered_scaled,
        first_inverse_deviation,
        first_norm_gain.astype(jnp.float32),
    )
    grad_attn_full = lax.all_gather(
        first_residual_gradient.astype(jnp.bfloat16), "tp", axis=0, tiled=True
    )
    grad_out_bias = jnp.sum(grad_attn_full, axis=0, dtype=jnp.float32)
    grad_out_weight = contract_first(grad_attn_full, mixed_rows)
    grad_mixed = jnp.dot(grad_attn_full, out_weight, preferred_element_type=jnp.float32).astype(
        jnp.bfloat16
    )

    def attend_back(carry, inputs):
        key_grad, value_grad = carry
        query_block, seg_block, total_block, grad_block = inputs
        scores = masked_scores(query_block, seg_block)
        shares = jnp.exp(scores - total_block[:, :, None])
        grad_shares = jnp.einsum(
            "qhd,khd->hqk", grad_block, value_heads, preferred_element_type=jnp.float32
        )
        centre = jnp.sum(shares * grad_shares, axis=-1, keepdims=True)
        grad_scores = (shares * (grad_shares - centre)).astype(jnp.bfloat16)
        query_grad = (
            jnp.einsum("hqk,khd->qhd", grad_scores, key_heads, preferred_element_type=jnp.float32)
            * scale
        )
        key_grad = (
            key_grad
            + jnp.einsum(
                "hqk,qhd->khd", grad_scores, query_block, preferred_element_type=jnp.float32
            )
            * scale
        )
        value_grad = value_grad + jnp.einsum(
            "hqk,qhd->khd",
            shares.astype(jnp.bfloat16),
            grad_block,
            preferred_element_type=jnp.float32,
        )
        return ((key_grad, value_grad), query_grad.astype(jnp.bfloat16).reshape(block, width))

    zero_heads = jnp.zeros((group_rows, heads, HD), jnp.float32)
    (key_grad, value_grad), query_grads = lax.scan(
        attend_back,
        (zero_heads, zero_heads),
        (query_blocks, seg_blocks, log_totals, grad_mixed.reshape(blocks, block, heads, HD)),
    )
    grad_query = query_grads.reshape(group_rows, width)
    grad_key = key_grad.astype(jnp.bfloat16).reshape(group_rows, width)
    grad_value = value_grad.astype(jnp.bfloat16).reshape(group_rows, width)
    grad_query_weight = contract_first(input_full, grad_query)
    grad_key_weight = contract_first(input_full, grad_key)
    grad_value_weight = contract_first(input_full, grad_value)
    total = contract_last(grad_query, query_weight)
    total = total + contract_last(grad_key, key_weight)
    back_term = lax.psum_scatter(
        (total + contract_last(grad_value, value_weight)).astype(jnp.bfloat16),
        "tp",
        scatter_dimension=0,
        tiled=True,
    ).astype(jnp.float32)
    grad_tokens = first_residual_gradient + back_term
    empty_model = jnp.zeros((query_bias.shape[0],), jnp.float32)
    query_bias_grad = lax.dynamic_update_slice_in_dim(
        empty_model, jnp.sum(grad_query, axis=0, dtype=jnp.float32), tp_index * width, 0
    )
    value_bias_grad = lax.dynamic_update_slice_in_dim(
        empty_model, jnp.sum(grad_value, axis=0, dtype=jnp.float32), tp_index * width, 0
    )
    up_bias_grad = lax.dynamic_update_slice_in_dim(
        jnp.zeros((up_bias.shape[0],), jnp.float32), grad_up_bias, tp_index * hidden_width, 0
    )
    (
        query_bias_grad,
        value_bias_grad,
        up_bias_grad,
        first_gain_gradient,
        grad_shift_one,
        second_gain_gradient,
        grad_shift_two,
    ) = lax.psum(
        (
            query_bias_grad,
            value_bias_grad,
            up_bias_grad,
            first_gain_gradient,
            grad_shift_one,
            second_gain_gradient,
            grad_shift_two,
        ),
        "tp",
    )
    owned = (
        lax.psum_scatter(grad_query_weight, "dp", scatter_dimension=0, tiled=True),
        lax.psum_scatter(grad_key_weight, "dp", scatter_dimension=0, tiled=True),
        lax.psum_scatter(grad_value_weight, "dp", scatter_dimension=0, tiled=True),
        lax.psum_scatter(grad_out_weight, "dp", scatter_dimension=0, tiled=True),
        lax.psum_scatter(grad_up_weight, "dp", scatter_dimension=0, tiled=True),
        lax.psum_scatter(grad_down_weight, "dp", scatter_dimension=0, tiled=True),
        lax.psum_scatter(query_bias_grad, "dp", scatter_dimension=0, tiled=True),
        lax.psum_scatter(value_bias_grad, "dp", scatter_dimension=0, tiled=True),
        lax.psum_scatter(grad_out_bias, "dp", scatter_dimension=0, tiled=True),
        lax.psum_scatter(first_gain_gradient, "dp", scatter_dimension=0, tiled=True),
        lax.psum_scatter(grad_shift_one, "dp", scatter_dimension=0, tiled=True),
        lax.psum_scatter(up_bias_grad, "dp", scatter_dimension=0, tiled=True),
        lax.psum_scatter(grad_down_bias, "dp", scatter_dimension=0, tiled=True),
        lax.psum_scatter(second_gain_gradient, "dp", scatter_dimension=0, tiled=True),
        lax.psum_scatter(grad_shift_two, "dp", scatter_dimension=0, tiled=True),
    )
    return (
        encoder_output,
        grad_tokens,
        owned[0],
        owned[1],
        owned[2],
        owned[6],
        owned[7],
        owned[3],
        owned[8],
        owned[9],
        owned[10],
        owned[4],
        owned[11],
        owned[5],
        owned[12],
        owned[13],
        owned[14],
    )


def solution(mesh):
    in_specs = (
        P(("dp", "tp"), None),
        P("dp", "tp"),
        P("dp", "tp"),
        P("dp", "tp"),
        P("dp"),
        P("dp"),
        P("dp", "tp"),
        P("dp"),
        P("dp"),
        P("dp"),
        P("dp", "tp"),
        P("dp"),
        P("dp", "tp"),
        P("dp"),
        P("dp"),
        P("dp"),
        P(),
        P(),
        P(("dp", "tp"), None),
    )
    out_specs = (
        P(("dp", "tp"), None),
        P(("dp", "tp"), None),
        P("dp", "tp"),
        P("dp", "tp"),
        P("dp", "tp"),
        P("dp"),
        P("dp"),
        P("dp", "tp"),
        P("dp"),
        P("dp"),
        P("dp"),
        P("dp", "tp"),
        P("dp"),
        P("dp", "tp"),
        P("dp"),
        P("dp"),
        P("dp"),
    )
    return jax.shard_map(body, mesh=mesh, in_specs=in_specs, out_specs=out_specs, check_vma=False)
```

profile of v0, /device:TPU:0, one launch (start us, length us, event | category | flops | bytes accessed | tf_op | source)
XLA Modules:
  0.0 1452.7 jit_solution(7568280337318745953)
XLA Ops:
  18.3 27.4 %all-reduce.19 = (bf16[768]{0:T(1024)(128)(2,1)S(1)}, bf16[768]{0:T(1024)(128)(2,1)S(1)}, bf16[768]{0:T(1024)(128)(2,1)}, bf16[768]{0:T(1024)(128)(2,1)}, bf16[7...) all-reduce(bf16[768]{0:T(1024)(128)(2,1)S(1)} %dynamic-update-slice, ...), channel_id=1, replica_groups=mesh['dp'=8,'tp'=4] {'dp'}, use_global_device_ids=true, to_apply=%add | all-reduce | flops 6144 | bytes 24576
  45.6 8.8 all_gather.66
  54.5 9.3 all_gather.68
  63.7 8.8 all_gather.69
  72.6 10.4 all_gather.71
  85.1 4.4 all-gather.8.cloned.1.call-done
  89.6 4.5 fusion.56
  103.4 72.3 %while.28 = (s32[]{:T(128)}, bf16[5,512,192]{1,2,0:T(8,128)(2,1)}, f32[5,3,512]{2,1,0:T(4,128)S(1)}, s32[5,512]{1,0:T(8,128)S(1)}, bf16[5,512,3,64]{1,3,2,0:T(8,...) while((s32[]{:T(128)}, bf16[5,512,192]{1,2,0:T(8,128)(2,1)}, ...), condition=%wide.region_4.5_spmd.clone, body=%wide.region_1.4_spmd.clone.sunk | while | flops 1055231488 | bytes 55263352 | solution.py:177
  108.1 4.3 fusion.150
  112.5 4.7 fusion.151
  122.6 4.3 fusion.150
  126.9 4.7 fusion.151
  141.4 4.7 fusion.151
  155.8 4.7 fusion.151
  166.0 4.3 fusion.150
  170.3 4.7 fusion.151
  178.5 5.6 fusion.75
  185.3 133.9 %reduce-scatter.17.cloned.1.call-done = f32[640,768]{1,0:T(8,128)} async-done(((f32[2560,768]{1,0:T(8,128)}), f32[640,768]{1,0:T(8,128)}) %reduce-scatter.17.cloned.1.call-update) | async-done | bytes 1966096 | tf_op jit(solution)/shard_map/reduce_scatter | solution.py:179
  323.7 8.9 all-gather
  332.7 67.2 %all-gather.10.cloned.1.call-done = bf16[2560,768]{1,0:T(8,128)(2,1)} async-done(((bf16[640,768]{1,0:T(8,128)(2,1)}), bf16[2560,768]{1,0:T(8,128)(2,1)}) %all-gather.10.cloned.1.call-update) | async-done | bytes 3932176 | tf_op jit(solution)/shard_map/all_gather | solution.py:187
  399.9 22.3 %fusion.42 = (bf16[2560,768]{1,0:T(8,128)(2,1)}, f32[2560,768]{1,0:T(8,128)}) fusion(f32[768]{0:T(1024)S(1)} %dynamic-slice_convert_fusion, bf16[2560,768]{1,0:T(8,128)(2,1)} %all-gather.10.cloned.1.call-done, bf16[768,768]{1,0:T(8,128)(2,1)} %all-gather.12.cloned.1.call-done), kind=kOutput, calls=%fused_computation.56 | convolution fusion | flops 3149660160 | bytes 16911360 | tf_op jit(solution)/shard_map/dot_general | solution.py:188
  424.0 8.9 fusion.76
  433.6 135.6 %reduce-scatter.19.cloned.1.call-done = f32[640,768]{1,0:T(8,128)} async-done(((f32[2560,768]{1,0:T(8,128)}), f32[640,768]{1,0:T(8,128)}) %reduce-scatter.19.cloned.1.call-update) | async-done | bytes 1966096 | tf_op jit(solution)/shard_map/reduce_scatter | solution.py:190
  575.1 77.0 %all-gather.16.cloned.1.call-done = bf16[2560,768]{1,0:T(8,128)(2,1)} async-done(((bf16[640,768]{1,0:T(8,128)(2,1)}), bf16[2560,768]{1,0:T(8,128)(2,1)}) %all-gather.16.cloned.1.call-update) | async-done | bytes 3932176 | tf_op jit(solution)/shard_map/all_gather | solution.py:243
  652.1 9.7 convert_reduce_fusion.1
  663.8 5.4 fusion.77
  669.8 134.2 %reduce-scatter.21.cloned.1.call-done = f32[640,768]{1,0:T(8,128)} async-done(((f32[2560,768]{1,0:T(8,128)}), f32[640,768]{1,0:T(8,128)}) %reduce-scatter.21.cloned.1.call-update) | async-done | bytes 1966096 | tf_op jit(solution)/shard_map/reduce_scatter | solution.py:252
  804.0 5.6 multiply_reduce_fusion.1
  812.2 76.9 %all-gather.18.cloned.1.call-done = bf16[2560,768]{1,0:T(8,128)(2,1)} async-done(((bf16[640,768]{1,0:T(8,128)(2,1)}), bf16[2560,768]{1,0:T(8,128)(2,1)}) %all-gather.18.cloned.1.call-update) | async-done | bytes 3932176 | tf_op jit(solution)/shard_map/all_gather | solution.py:263
  898.4 215.4 %while.29 = (s32[]{:T(128)}, f32[2560,3,64]{0,2,1:T(8,128)}, f32[2560,3,64]{0,2,1:T(8,128)}, bf16[5,512,192]{1,2,0:T(8,128)(2,1)}, bf16[5,512,3,64]{1,3,2,0:T(8,...) while((s32[]{:T(128)}, f32[2560,3,64]{0,2,1:T(8,128)}, ...), condition=%wide.region_18.19_spmd.clone, body=%wide.region_16.18_spmd.clone.sunk | while | flops 2555940352 | bytes 180019440 | solution.py:302
  899.9 8.7 fusion.161
  908.6 9.1 multiply_reduce_fusion.7
  917.7 9.5 multiply_convert_fusion.2
  931.2 5.8 fusion.165
  942.4 8.7 fusion.161
  951.1 9.1 multiply_reduce_fusion.7
  960.2 9.5 multiply_convert_fusion.2
  969.8 4.6 fusion.164
  974.4 5.9 fusion.165
  985.6 8.7 fusion.161
  994.3 9.1 multiply_reduce_fusion.7
  1003.4 9.5 multiply_convert_fusion.2
  1013.0 4.6 fusion.164
  1017.6 5.9 fusion.165
  1028.9 8.7 fusion.161
  1037.5 9.1 multiply_reduce_fusion.7
  1046.7 9.5 multiply_convert_fusion.2
  1056.2 4.6 fusion.164
  1060.8 5.8 fusion.165
  1072.1 8.7 fusion.161
  1080.8 9.1 multiply_reduce_fusion.7
  1089.9 9.5 multiply_convert_fusion.2
  1099.4 4.6 fusion.164
  1104.1 5.9 fusion.165
  1126.3 8.0 fusion.81
  1134.4 8.0 fusion.82
  1168.5 25.8 %all-reduce.17 = (f32[768]{0:T(1024)S(1)}, f32[768]{0:T(1024)S(1)}, f32[768]{0:T(1024)S(1)}, f32[768]{0:T(1024)S(1)}, f32[768]{0:T(1024)S(1)}, /*index=5*/f32[30...) all-reduce(f32[768]{0:T(1024)S(1)} %dynamic_update_slice.20, ...), channel_id=9, replica_groups=mesh['dp'=8,'tp'=4] {'dp'}, use_global_device_ids=true, to_apply=%region_25.26.clone | all-reduce | flops 9216 | bytes 73728
  1196.0 9.1 all-reduce.18
  1207.7 36.4 %reduce-scatter.27.cloned.1.call-done = f32[96,768]{1,0:T(8,128)} async-done(((f32[768,768]{1,0:T(8,128)}), f32[96,768]{1,0:T(8,128)}) %reduce-scatter.27.cloned.1.call-update) | async-done | bytes 294928 | tf_op jit(solution)/shard_map/reduce_scatter | solution.py:357
  1244.1 46.3 %reduce-scatter.29.cloned.1.call-done = f32[96,768]{1,0:T(8,128)} async-done(((f32[768,768]{1,0:T(8,128)}), f32[96,768]{1,0:T(8,128)}) %reduce-scatter.29.cloned.1.call-update) | async-done | bytes 294928 | tf_op jit(solution)/shard_map/reduce_scatter | solution.py:358
  1290.4 38.7 %reduce-scatter.25.cloned.1.call-done = f32[96,192]{1,0:T(8,128)} async-done(((f32[768,192]{1,0:T(8,128)}), f32[96,192]{1,0:T(8,128)}) %reduce-scatter.25.cloned.1.call-update) | async-done | bytes 73744 | tf_op jit(solution)/shard_map/reduce_scatter | solution.py:356
  1329.1 38.7 %reduce-scatter.31.cloned.1.call-done = f32[96,192]{1,0:T(8,128)} async-done(((f32[768,192]{1,0:T(8,128)}), f32[96,192]{1,0:T(8,128)}) %reduce-scatter.31.cloned.1.call-update) | async-done | bytes 73744
  1367.8 38.6 %reduce-scatter.33.cloned.1.call-done = f32[96,192]{1,0:T(8,128)} async-done(((f32[768,192]{1,0:T(8,128)}), f32[96,192]{1,0:T(8,128)}) %reduce-scatter.33.cloned.1.call-update) | async-done | bytes 73744
  1406.4 38.7 %reduce-scatter.35.cloned.1.call-done = f32[96,192]{1,0:T(8,128)} async-done(((f32[768,192]{1,0:T(8,128)}), f32[96,192]{1,0:T(8,128)}) %reduce-scatter.35.cloned.1.call-update) | async-done | bytes 73744
  (283 shorter events, 159.9 us)
Async XLA Ops:
  8.0 81.6 %all-gather.8.cloned.1.call-start = ((), (), s32[]{:S(2)}) async-start(), calls=%async_computation.10 | async-start | bytes 4915200 | tf_op jit(solution)/shard_map/all_gather | solution.py:141
  8.8 310.4 %reduce-scatter.17.cloned.1.call-start = ((), (), s32[]{:S(2)}) async-start(), calls=%async_computation.11 | async-start | bytes 9830400 | tf_op jit(solution)/shard_map/reduce_scatter | solution.py:179
  54.5 39.6 %copy-start.19 = (bf16[768,192]{1,0:T(8,128)(2,1)}, bf16[768,192]{1,0:T(8,128)(2,1)S(1)}, u32[]{:S(2)}) copy-start(bf16[768,192]{1,0:T(8,128)(2,1)S(1)} %all_gather.66) | copy-start | bytes 884740
  63.7 33.5 %copy-start.14 = (bf16[768,192]{1,0:T(8,128)(2,1)}, bf16[768,192]{1,0:T(8,128)(2,1)S(1)}, u32[]{:S(2)}) copy-start(bf16[768,192]{1,0:T(8,128)(2,1)S(1)} %all_gather.68) | copy-start | bytes 884740
  72.6 28.4 %copy-start.17 = (bf16[768,192]{1,0:T(8,128)(2,1)}, bf16[768,192]{1,0:T(8,128)(2,1)S(1)}, u32[]{:S(2)}) copy-start(bf16[768,192]{1,0:T(8,128)(2,1)S(1)} %all_gather.69) | copy-start | bytes 884740
  97.2 3.7 copy-start.3
  175.7 0.9 copy-start.10
  176.7 7.5 copy-start.5
  178.5 5.6 copy-start.7
  184.1 1.1 copy-start.30
  184.1 1.1 copy-start.29
  184.2 1.1 copy-start.28
  184.2 148.5 %all-gather.12.cloned.1.call-start = ((), (), s32[]{:S(2)}) async-start(), calls=%async_computation.13 | async-start | bytes 1327104 | tf_op jit(solution)/shard_map/all_gather | solution.py:92
  184.8 215.2 %all-gather.10.cloned.1.call-start = ((), (), s32[]{:S(2)}) async-start(), calls=%async_computation.12 | async-start | bytes 4915200 | tf_op jit(solution)/shard_map/all_gather | solution.py:187
  321.3 2.4 copy-start.31
  323.0 101.0 %all-gather.14.cloned.1.call-start = ((), (), s32[]{:S(2)}) async-start(), calls=%async_computation.14 | async-start | bytes 1327104 | tf_op jit(solution)/shard_map/all_gather | solution.py:93
  323.6 245.7 %reduce-scatter.19.cloned.1.call-start = ((), (), s32[]{:S(2)}) async-start(), calls=%async_computation.15 | async-start | bytes 9830400 | tf_op jit(solution)/shard_map/reduce_scatter | solution.py:190
  432.9 0.7 copy-start.27
  432.9 0.7 copy-start.26
  432.9 219.2 %all-gather.16.cloned.1.call-start = ((), (), s32[]{:S(2)}) async-start(), calls=%async_computation.16 | async-start | bytes 4915200 | tf_op jit(solution)/shard_map/all_gather | solution.py:243
  569.3 2.7 copy-start.11
  571.6 1.9 copy-start.4
  575.0 229.0 %reduce-scatter.21.cloned.1.call-start = ((), (), s32[]{:S(2)}) async-start(), calls=%async_computation.17 | async-start | bytes 9830400 | tf_op jit(solution)/shard_map/reduce_scatter | solution.py:252
  652.1 11.6 copy-start.32
  661.8 2.0 copy-start.33
  669.2 0.7 copy-start.25
  669.2 219.9 %all-gather.18.cloned.1.call-start = ((), (), s32[]{:S(2)}) async-start(), calls=%async_computation.18 | async-start | bytes 4915200 | tf_op jit(solution)/shard_map/all_gather | solution.py:263
  809.7 79.4 %copy-start.16 = (bf16[768,192]{1,0:T(8,128)(2,1)S(1)}, bf16[768,192]{1,0:T(8,128)(2,1)}, u32[]{:S(2)}) copy-start(bf16[768,192]{1,0:T(8,128)(2,1)} %all_gather.71) | copy-start | bytes 884740
  812.0 393.1 %reduce-scatter.23.cloned.1.call-start = ((), (), s32[]{:S(2)}) async-start(), calls=%async_computation.19 | async-start | bytes 4915200 | tf_op jit(solution)/shard_map/reduce_scatter | solution.py:315
  892.6 5.8 copy-start.6
  927.3 9.8 copy-start.1
  931.2 5.9 copy-start
  939.6 1.3 copy-start.2
  969.8 10.5 copy-start.1
  974.4 5.9 copy-start
  982.8 1.3 copy-start.2
  1013.0 10.5 copy-start.1
  1017.6 5.9 copy-start
  1026.0 1.4 copy-start.2
  1056.2 10.5 copy-start.1
  1060.8 5.9 copy-start
  1069.3 1.3 copy-start.2
  1099.4 10.5 copy-start.1
  1104.1 5.9 copy-start
  1112.5 1.4 copy-start.2
  1117.2 4.5 copy-start.9
  1119.5 2.3 copy-start.15
  1121.8 1.3 copy-start.18
  1126.2 117.9 %reduce-scatter.27.cloned.1.call-start = ((), (), s32[]{:S(2)}) async-start(), calls=%async_computation.21 | async-start | bytes 2654208 | tf_op jit(solution)/shard_map/reduce_scatter | solution.py:357
  1134.3 8.2 copy-start.8
  1134.3 156.1 %reduce-scatter.29.cloned.1.call-start = ((), (), s32[]{:S(2)}) async-start(), calls=%async_computation.22 | async-start | bytes 2654208 | tf_op jit(solution)/shard_map/reduce_scatter | solution.py:358
  1142.4 186.7 %reduce-scatter.25.cloned.1.call-start = ((), (), s32[]{:S(2)}) async-start(), calls=%async_computation.20 | async-start | bytes 884736 | tf_op jit(solution)/shard_map/reduce_scatter | solution.py:356
  1146.8 221.0 %reduce-scatter.31.cloned.1.call-start = ((), (), s32[]{:S(2)}) async-start(), calls=%async_computation.23 | async-start | bytes 884736
  1151.8 254.6 %reduce-scatter.33.cloned.1.call-start = ((), (), s32[]{:S(2)}) async-start(), calls=%async_computation.24 | async-start | bytes 884736
  1156.0 289.1 %reduce-scatter.35.cloned.1.call-start = ((), (), s32[]{:S(2)}) async-start(), calls=%async_computation.25 | async-start | bytes 884736
  1160.5 4.2 copy-start.24
  1160.5 4.5 copy-start.12
  1161.7 6.8 copy-start.20
  1161.7 6.8 copy-start.21
  1161.7 6.8 copy-start.22
  1161.7 6.8 copy-start.23
  1161.7 43.4 %copy-start.13 = (f32[640,768]{1,0:T(8,128)S(1)}, f32[640,768]{1,0:T(8,128)}, u32[]{:S(2)}) copy-start(f32[640,768]{1,0:T(8,128)} %get-tuple-element.363) | copy-start | bytes 5898244
Sparse Core Ops, SparseCore 0:
  10.4 79.1 all-gather.7
  184.3 134.8 reduce-scatter.16
  575.2 76.9 all-gather.15
  812.1 76.9 all-gather.17
  1126.3 71.1 reduce-scatter.22
  1201.3 42.7 reduce-scatter.26
  1248.0 42.3 reduce-scatter.28
  1294.1 34.9 reduce-scatter.24
  1332.8 34.9 reduce-scatter.30
  1371.4 34.9 reduce-scatter.32
  1410.1 34.9 reduce-scatter.34
Sparse Core Ops, SparseCore 1:
  186.6 22.3 all-gather.11
  323.1 76.8 all-gather.9
  401.7 22.3 all-gather.13
  433.0 136.2 reduce-scatter.18
  669.3 134.7 reduce-scatter.20
where the time goes:
time: 1460 us; the launch traced here: 1450 us
  waiting for transfers between devices  870 us (60%)
  matrix products  295 us (20%)
  other arithmetic  116 us (8%)
  blocking collectives  109 us (7%)
  local copies, waits for them, and re-layouts  42.9 us (3%)
  between operations  18.4 us (1%)
    reduce_scatter x1, waiting for transfers between devices, body(): lax.psum_scatter(contract_last(hidden, down_weight), 'tp', scatter_dimens...  136 us
    reduce_scatter x1, waiting for transfers between devices, body(): lax.psum_scatter(contract_last(grad_pre, up_weight), 'tp', scatter_dimens...  134 us
    reduce_scatter x1, waiting for transfers between devices, body(): lax.psum_scatter(contract_last(mixed_rows, out_weight), 'tp', scatter_dim...  134 us
    unnamed x19, waiting for transfers between devices  118 us
    all_gather x1, waiting for transfers between devices, body(): lax.all_gather(second_residual_gradient.astype(jnp.bfloat16), 'tp', axis=...  77 us
    all_gather x1, waiting for transfers between devices, body(): lax.all_gather(first_residual_gradient.astype(jnp.bfloat16), 'tp', axis=0...  76.9 us
    all_gather x1, waiting for transfers between devices, body(): lax.all_gather(normalized_rows.astype(jnp.bfloat16), 'tp', axis=0, tiled=...  67.2 us
    dot_general x10, matrix products, masked_scores(): jnp.einsum('qhd,khd->hqk', query_block, key_heads, preferred_element_type...  61.8 us
  transfers between devices with their start and end apart: 16, of which 14 were waited for; matrix products, arithmetic and copies ran while one was open for 6% of the time, Pallas kernels for 0%

commit v1 on v0

--- a/solution.py
+++ b/solution.py
@@ -7,6 +7,27 @@
 EPS = 1e-05
 SQRT_HALF = 0.7071067811865476
 INV_ROOT_TAU = 0.3989422804014327
+
+
+def gather_around(value, axis, dim):
+    peers, here, span = (lax.axis_size(axis), lax.axis_index(axis), value.shape[dim])
+    right = [(i, (i + 1) % peers) for i in range(peers)]
+    downward = [(i, (i - 1) % peers) for i in range(peers)]
+    filled = jnp.zeros((*value.shape[:dim], peers * span, *value.shape[dim + 1 :]), value.dtype)
+    filled = lax.dynamic_update_slice_in_dim(filled, value, here * span, axis=dim)
+    from_left = from_right = value
+    half = peers // 2
+    for step in range(1, half + 1):
+        from_left = lax.ppermute(from_left, axis, right)
+        filled = lax.dynamic_update_slice_in_dim(
+            filled, from_left, (here - step) % peers * span, axis=dim
+        )
+        if step < peers - half:
+            from_right = lax.ppermute(from_right, axis, downward)
+            filled = lax.dynamic_update_slice_in_dim(
+                filled, from_right, (here + step) % peers * span, axis=dim
+            )
+    return filled
 
 
 def normalize_layer(resid):
@@ -184,7 +205,7 @@
     normalized_rows = first_centered_scaled * first_norm_gain.astype(
         jnp.float32
     ) + first_norm_shift.astype(jnp.float32)
-    normed_full = lax.all_gather(normalized_rows.astype(jnp.bfloat16), "tp", axis=0, tiled=True)
+    normed_full = gather_around(normalized_rows.astype(jnp.bfloat16), "tp", 0)
     pre_act = jnp.dot(normed_full, up_weight, preferred_element_type=jnp.float32) + own_up_bias
     hidden = jax.nn.gelu(pre_act, approximate=False).astype(jnp.bfloat16)
     feedforward_term = lax.psum_scatter(

time: 1460 us -> 1450 us (level)
  waiting for transfers between devices: 870 us -> 832 us
  starting transfers between devices: 1.49 us -> 23.9 us
    all_gather x1 -> x0, waiting for transfers between devices: 67.2 us -> none  [body(): lax.all_gather(normalized_rows.astype(jnp.bfloat16), 'tp', axis=0, tiled=...]
    ppermute x0 -> x3, waiting for transfers between devices: none -> 31.7 us  [the longest x2 31.7 us: gather_around(): from_left = lax.ppermute(from_left, axis, right)]
    ppermute x0 -> x3, starting transfers between devices: none -> 22.4 us  [the longest x2 20 us: gather_around(): from_left = lax.ppermute(from_left, axis, right)]
    unnamed x19 -> x18, waiting for transfers between devices: 118 us -> 117 us
  transfers between devices with their start and end apart: 16 -> 18, of which waited for: 14 -> 14; matrix products, arithmetic and copies ran while one was open for 6% -> 6% of each run, Pallas kernels for 0% -> 0%
where the time goes in v1:
time: 1450 us
  waiting for transfers between devices  832 us (57%)
  matrix products  294 us (20%)
  other arithmetic  116 us (8%)
  blocking collectives  108 us (7%)
  local copies, waits for them, and re-layouts  52.6 us (4%)
  starting transfers between devices  23.9 us (2%)
  between operations  18.4 us (1%)
    reduce_scatter x1, waiting for transfers between devices, body(): lax.psum_scatter(contract_last(hidden, down_weight), 'tp', scatter_dimens...  135 us
    reduce_scatter x1, waiting for transfers between devices, body(): lax.psum_scatter(contract_last(grad_pre, up_weight), 'tp', scatter_dimens...  134 us
    reduce_scatter x1, waiting for transfers between devices, body(): lax.psum_scatter(contract_last(mixed_rows, out_weight), 'tp', scatter_dim...  134 us
    unnamed x18, waiting for transfers between devices  117 us
    all_gather x1, waiting for transfers between devices, body(): lax.all_gather(first_residual_gradient.astype(jnp.bfloat16), 'tp', axis=0...  77 us
    all_gather x1, waiting for transfers between devices, body(): lax.all_gather(second_residual_gradient.astype(jnp.bfloat16), 'tp', axis=...  76.9 us
    dot_general x10, matrix products, masked_scores(): jnp.einsum('qhd,khd->hqk', query_block, key_heads, preferred_element_type...  61.8 us
    unnamed x2, blocking collectives  53.1 us
  transfers between devices with their start and end apart: 18, of which 14 were waited for; matrix products, arithmetic and copies ran while one was open for 6% of the time, Pallas kernels for 0%

profile of v1, /device:TPU:0, one launch (start us, length us, event | category | flops | bytes accessed | tf_op | source)
XLA Modules:
  0.0 1445.5 jit_solution(10072454468113163312)
XLA Ops:
  18.3 27.4 %all-reduce.19 = (bf16[768]{0:T(1024)(128)(2,1)S(1)}, bf16[768]{0:T(1024)(128)(2,1)S(1)}, bf16[768]{0:T(1024)(128)(2,1)}, bf16[768]{0:T(1024)(128)(2,1)}, bf16[7...) all-reduce(bf16[768]{0:T(1024)(128)(2,1)S(1)} %dynamic-update-slice, ...), channel_id=1, replica_groups=mesh['dp'=8,'tp'=4] {'dp'}, use_global_device_ids=true, to_apply=%add | all-reduce | flops 6144 | bytes 24576
  45.6 8.8 all_gather.63
  54.5 9.3 all_gather.65
  63.7 8.8 all_gather.66
  72.6 10.4 all_gather.68
  85.1 4.4 all-gather.7.cloned.1.call-done
  103.3 72.3 %while.28 = (s32[]{:T(128)}, bf16[5,512,192]{1,2,0:T(8,128)(2,1)}, f32[5,3,512]{2,1,0:T(4,128)S(1)}, s32[5,512]{1,0:T(8,128)S(1)}, bf16[5,512,3,64]{1,3,2,0:T(8,...) while((s32[]{:T(128)}, bf16[5,512,192]{1,2,0:T(8,128)(2,1)}, ...), condition=%wide.region_4.5_spmd.clone, body=%wide.region_1.4_spmd.clone.sunk | while | flops 1055231488 | bytes 55263352 | solution.py:198
  108.1 4.3 fusion.151
  112.4 4.7 fusion.152
  122.5 4.3 fusion.151
  126.8 4.7 fusion.152
  141.3 4.7 fusion.152
  155.8 4.7 fusion.152
  170.2 4.7 fusion.152
  178.5 5.6 fusion.76
  185.3 133.8 %reduce-scatter.17.cloned.1.call-done = f32[640,768]{1,0:T(8,128)} async-done(((f32[2560,768]{1,0:T(8,128)}), f32[640,768]{1,0:T(8,128)}) %reduce-scatter.17.cloned.1.call-update) | async-done | bytes 1966096 | tf_op jit(solution)/shard_map/reduce_scatter | solution.py:200
  329.3 23.0 %collective-permute-done = bf16[640,768]{1,0:T(8,128)(2,1)} collective-permute-done((bf16[640,768]{1,0:T(8,128)(2,1)}, bf16[640,768]{1,0:T(8,128)(2,1)}, u32[]{:S(2)}, u32[]{:S(2)}) %collective-permute-start) | collective-permute-done | bytes 983072 | tf_op jit(solution)/shard_map/ppermute | solution.py:21
  352.3 18.6 %collective-permute-start.2 = (bf16[640,768]{1,0:T(8,128)(2,1)}, bf16[640,768]{1,0:T(8,128)(2,1)}, u32[]{:S(2)}, u32[]{:S(2)}) collective-permute-start(bf16[640,768]{1,0:T(8,128)(2,1)} %collective-permute-done), channel_id=1, source_target_pairs={{0,1},{1,2},{2,3},{3,0},{4,5},{5,6},{6,7},{7,4},{8,9},{9,10},{10,1... | collective-permute-start | bytes 2949128 | tf_op jit(solution)/shard_map/ppermute | solution.py:21
  371.0 8.9 all-gather
  384.5 8.7 collective-permute-done.2
  395.5 22.3 %fusion.42 = (bf16[2560,768]{1,0:T(8,128)(2,1)}, f32[2560,768]{1,0:T(8,128)}) fusion(f32[768]{0:T(1024)S(1)} %dynamic-slice_convert_fusion, bf16[2560,768]{1,0:T(8,128)(2,1)} %constant_dynamic-update-slice_fusion, bf16[768,768]{1,0:T(8,128)(2,1)} %all-gather.9.cloned.1.call-done), kind=kOutput, calls=%fused_computation.56 | convolution fusion | flops 3149660160 | bytes 16911360 | tf_op jit(solution)/shard_map/dot_general | solution.py:209
  417.7 8.9 fusion.77
  427.3 134.9 %reduce-scatter.19.cloned.1.call-done = f32[640,768]{1,0:T(8,128)} async-done(((f32[2560,768]{1,0:T(8,128)}), f32[640,768]{1,0:T(8,128)}) %reduce-scatter.19.cloned.1.call-update) | async-done | bytes 1966096 | tf_op jit(solution)/shard_map/reduce_scatter | solution.py:211
  568.2 76.9 %all-gather.13.cloned.1.call-done = bf16[2560,768]{1,0:T(8,128)(2,1)} async-done(((bf16[640,768]{1,0:T(8,128)(2,1)}), bf16[2560,768]{1,0:T(8,128)(2,1)}) %all-gather.13.cloned.1.call-update) | async-done | bytes 3932176 | tf_op jit(solution)/shard_map/all_gather | solution.py:264
  645.0 9.7 convert_reduce_fusion.1
  656.6 5.4 fusion.78
  662.7 134.3 %reduce-scatter.21.cloned.1.call-done = f32[640,768]{1,0:T(8,128)} async-done(((f32[2560,768]{1,0:T(8,128)}), f32[640,768]{1,0:T(8,128)}) %reduce-scatter.21.cloned.1.call-update) | async-done | bytes 1966096 | tf_op jit(solution)/shard_map/reduce_scatter | solution.py:273
  797.0 5.6 multiply_reduce_fusion.1
  804.9 77.0 %all-gather.15.cloned.1.call-done = bf16[2560,768]{1,0:T(8,128)(2,1)} async-done(((bf16[640,768]{1,0:T(8,128)(2,1)}), bf16[2560,768]{1,0:T(8,128)(2,1)}) %all-gather.15.cloned.1.call-update) | async-done | bytes 3932176 | tf_op jit(solution)/shard_map/all_gather | solution.py:284
  891.3 215.4 %while.29 = (s32[]{:T(128)}, f32[2560,3,64]{0,2,1:T(8,128)}, f32[2560,3,64]{0,2,1:T(8,128)}, bf16[5,512,192]{1,2,0:T(8,128)(2,1)}, bf16[5,512,3,64]{1,3,2,0:T(8,...) while((s32[]{:T(128)}, f32[2560,3,64]{0,2,1:T(8,128)}, ...), condition=%wide.region_18.19_spmd.clone, body=%wide.region_16.18_spmd.clone.sunk | while | flops 2555940352 | bytes 180019440 | solution.py:323
  892.8 8.7 fusion.162
  901.5 9.1 multiply_reduce_fusion.7
  910.6 9.5 multiply_convert_fusion.2
  924.1 5.9 fusion.166
  935.3 8.7 fusion.162
  944.0 9.1 multiply_reduce_fusion.7
  953.1 9.5 multiply_convert_fusion.2
  962.6 4.6 fusion.165
  967.3 5.9 fusion.166
  978.5 8.7 fusion.162
  987.2 9.1 multiply_reduce_fusion.7
  996.3 9.5 multiply_convert_fusion.2
  1005.8 4.6 fusion.165
  1010.5 5.9 fusion.166
  1021.7 8.7 fusion.162
  1030.4 9.1 multiply_reduce_fusion.7
  1039.5 9.5 multiply_convert_fusion.2
  1049.0 4.6 fusion.165
  1053.7 5.9 fusion.166
  1064.9 8.7 fusion.162
  1073.6 9.1 multiply_reduce_fusion.7
  1082.7 9.5 multiply_convert_fusion.2
  1092.3 4.6 fusion.165
  1096.9 5.9 fusion.166
  1119.1 8.0 fusion.82
  1127.2 8.1 fusion.83
  1161.4 25.8 %all-reduce.17 = (f32[768]{0:T(1024)S(1)}, f32[768]{0:T(1024)S(1)}, f32[768]{0:T(1024)S(1)}, f32[768]{0:T(1024)S(1)}, f32[768]{0:T(1024)S(1)}, /*index=5*/f32[30...) all-reduce(f32[768]{0:T(1024)S(1)} %dynamic_update_slice.36, ...), channel_id=9, replica_groups=mesh['dp'=8,'tp'=4] {'dp'}, use_global_device_ids=true, to_apply=%region_25.26.clone | all-reduce | flops 9216 | bytes 73728
  1188.9 9.1 all-reduce.18
  1200.6 36.5 %reduce-scatter.27.cloned.1.call-done = f32[96,768]{1,0:T(8,128)} async-done(((f32[768,768]{1,0:T(8,128)}), f32[96,768]{1,0:T(8,128)}) %reduce-scatter.27.cloned.1.call-update) | async-done | bytes 294928 | tf_op jit(solution)/shard_map/reduce_scatter | solution.py:378
  1237.1 46.3 %reduce-scatter.29.cloned.1.call-done = f32[96,768]{1,0:T(8,128)} async-done(((f32[768,768]{1,0:T(8,128)}), f32[96,768]{1,0:T(8,128)}) %reduce-scatter.29.cloned.1.call-update) | async-done | bytes 294928 | tf_op jit(solution)/shard_map/reduce_scatter | solution.py:379
  1283.4 38.6 %reduce-scatter.25.cloned.1.call-done = f32[96,192]{1,0:T(8,128)} async-done(((f32[768,192]{1,0:T(8,128)}), f32[96,192]{1,0:T(8,128)}) %reduce-scatter.25.cloned.1.call-update) | async-done | bytes 73744 | tf_op jit(solution)/shard_map/reduce_scatter | solution.py:377
  1322.0 38.7 %reduce-scatter.31.cloned.1.call-done = f32[96,192]{1,0:T(8,128)} async-done(((f32[768,192]{1,0:T(8,128)}), f32[96,192]{1,0:T(8,128)}) %reduce-scatter.31.cloned.1.call-update) | async-done | bytes 73744
  1360.7 38.5 %reduce-scatter.33.cloned.1.call-done = f32[96,192]{1,0:T(8,128)} async-done(((f32[768,192]{1,0:T(8,128)}), f32[96,192]{1,0:T(8,128)}) %reduce-scatter.33.cloned.1.call-update) | async-done | bytes 73744
  1399.2 38.7 %reduce-scatter.35.cloned.1.call-done = f32[96,192]{1,0:T(8,128)} async-done(((f32[768,192]{1,0:T(8,128)}), f32[96,192]{1,0:T(8,128)}) %reduce-scatter.35.cloned.1.call-update) | async-done | bytes 73744
  (290 shorter events, 179.3 us)
Async XLA Ops:
  8.0 81.6 %all-gather.7.cloned.1.call-start = ((), (), s32[]{:S(2)}) async-start(), calls=%async_computation.10 | async-start | bytes 4915200 | tf_op jit(solution)/shard_map/all_gather | solution.py:162
  8.8 310.3 %reduce-scatter.17.cloned.1.call-start = ((), (), s32[]{:S(2)}) async-start(), calls=%async_computation.11 | async-start | bytes 9830400 | tf_op jit(solution)/shard_map/reduce_scatter | solution.py:200
  54.5 38.7 %copy-start.19 = (bf16[768,192]{1,0:T(8,128)(2,1)}, bf16[768,192]{1,0:T(8,128)(2,1)S(1)}, u32[]{:S(2)}) copy-start(bf16[768,192]{1,0:T(8,128)(2,1)S(1)} %all_gather.63) | copy-start | bytes 884740
  63.7 33.4 %copy-start.14 = (bf16[768,192]{1,0:T(8,128)(2,1)}, bf16[768,192]{1,0:T(8,128)(2,1)S(1)}, u32[]{:S(2)}) copy-start(bf16[768,192]{1,0:T(8,128)(2,1)S(1)} %all_gather.65) | copy-start | bytes 884740
  72.6 28.3 %copy-start.17 = (bf16[768,192]{1,0:T(8,128)(2,1)}, bf16[768,192]{1,0:T(8,128)(2,1)S(1)}, u32[]{:S(2)}) copy-start(bf16[768,192]{1,0:T(8,128)(2,1)S(1)} %all_gather.66) | copy-start | bytes 884740
  97.1 3.7 copy-start.3
  175.6 0.9 copy-start.10
  176.6 7.5 copy-start.5
  178.5 5.6 copy-start.7
  184.1 1.1 copy-start.30
  184.1 1.2 copy-start.29
  184.1 1.2 copy-start.28
  184.1 211.4 %all-gather.9.cloned.1.call-start = ((), (), s32[]{:S(2)}) async-start(), calls=%async_computation.12 | async-start | bytes 1327104 | tf_op jit(solution)/shard_map/all_gather | solution.py:113
  184.7 233.1 %all-gather.11.cloned.1.call-start = ((), (), s32[]{:S(2)}) async-start(), calls=%async_computation.13 | async-start | bytes 1327104 | tf_op jit(solution)/shard_map/all_gather | solution.py:114
  321.6 49.4 %copy-start.31 = (bf16[384]{0:T(512)(128)(2,1)S(1)}, bf16[384]{0:T(512)(128)(2,1)}, u32[]{:S(2)}) copy-start(bf16[384]{0:T(512)(128)(2,1)} %param.34) | copy-start | bytes 2308
  325.5 26.8 %collective-permute-start = (bf16[640,768]{1,0:T(8,128)(2,1)}, bf16[640,768]{1,0:T(8,128)(2,1)}, u32[]{:S(2)}, u32[]{:S(2)}) collective-permute-start(bf16[640,768]{1,0:T(8,128)(2,1)} %get-tuple-element.368), channel_id=1, source_target_pairs={{0,1},{1,2},{2,3},{3,0},{4,5},{5,6},{6,7},{7,4},{8,9},{9,10},{10,1... | collective-permute-start | bytes 2949128 | tf_op jit(solution)/shard_map/ppermute | solution.py:21
  327.0 55.3 %collective-permute-start.1 = (bf16[640,768]{1,0:T(8,128)(2,1)}, bf16[640,768]{1,0:T(8,128)(2,1)}, u32[]{:S(2)}, u32[]{:S(2)}) collective-permute-start(bf16[640,768]{1,0:T(8,128)(2,1)} %get-tuple-element.368), channel_id=1, source_target_pairs={{0,3},{1,0},{2,1},{3,2},{4,7},{5,4},{6,5},{7,6},{8,11},{9,8},{10,9... | collective-permute-start | bytes 2949128 | tf_op jit(solution)/shard_map/ppermute | solution.py:26
  352.3 40.9 %collective-permute-start.2 = (bf16[640,768]{1,0:T(8,128)(2,1)}, bf16[640,768]{1,0:T(8,128)(2,1)}, u32[]{:S(2)}, u32[]{:S(2)}) collective-permute-start(bf16[640,768]{1,0:T(8,128)(2,1)} %collective-permute-done), channel_id=1, source_target_pairs={{0,1},{1,2},{2,3},{3,0},{4,5},{5,6},{6,7},{7,4},{8,9},{9,10},{10,1... | collective-permute-start | bytes 2949128 | tf_op jit(solution)/shard_map/ppermute | solution.py:21
  370.9 191.3 %reduce-scatter.19.cloned.1.call-start = ((), (), s32[]{:S(2)}) async-start(), calls=%async_computation.14 | async-start | bytes 9830400 | tf_op jit(solution)/shard_map/reduce_scatter | solution.py:211
  426.6 0.7 copy-start.27
  426.6 0.7 copy-start.26
  426.7 218.4 %all-gather.13.cloned.1.call-start = ((), (), s32[]{:S(2)}) async-start(), calls=%async_computation.15 | async-start | bytes 4915200 | tf_op jit(solution)/shard_map/all_gather | solution.py:264
  562.2 2.7 copy-start.11
  564.5 1.9 copy-start.4
  568.0 229.0 %reduce-scatter.21.cloned.1.call-start = ((), (), s32[]{:S(2)}) async-start(), calls=%async_computation.16 | async-start | bytes 9830400 | tf_op jit(solution)/shard_map/reduce_scatter | solution.py:273
  645.0 11.6 copy-start.32
  654.7 1.9 copy-start.33
  662.0 0.7 copy-start.25
  662.0 219.9 %all-gather.15.cloned.1.call-start = ((), (), s32[]{:S(2)}) async-start(), calls=%async_computation.17 | async-start | bytes 4915200 | tf_op jit(solution)/shard_map/all_gather | solution.py:284
  802.6 79.3 %copy-start.16 = (bf16[768,192]{1,0:T(8,128)(2,1)S(1)}, bf16[768,192]{1,0:T(8,128)(2,1)}, u32[]{:S(2)}) copy-start(bf16[768,192]{1,0:T(8,128)(2,1)} %all_gather.68) | copy-start | bytes 884740
  804.9 393.1 %reduce-scatter.23.cloned.1.call-start = ((), (), s32[]{:S(2)}) async-start(), calls=%async_computation.18 | async-start | bytes 4915200 | tf_op jit(solution)/shard_map/reduce_scatter | solution.py:336
  885.5 5.8 copy-start.6
  920.1 9.8 copy-start.1
  924.1 5.9 copy-start
  932.5 1.3 copy-start.2
  962.6 10.5 copy-start.1
  967.3 5.9 copy-start
  975.7 1.3 copy-start.2
  1005.8 10.5 copy-start.1
  1010.5 5.9 copy-start
  1018.9 1.4 copy-start.2
  1049.0 10.5 copy-start.1
  1053.7 5.9 copy-start
  1062.1 1.3 copy-start.2
  1092.3 10.5 copy-start.1
  1096.9 5.9 copy-start
  1105.3 1.4 copy-start.2
  1110.1 4.5 copy-start.9
  1112.3 2.3 copy-start.15
  1114.6 1.3 copy-start.18
  1119.1 118.1 %reduce-scatter.27.cloned.1.call-start = ((), (), s32[]{:S(2)}) async-start(), calls=%async_computation.20 | async-start | bytes 2654208 | tf_op jit(solution)/shard_map/reduce_scatter | solution.py:378
  1127.2 8.2 copy-start.8
  1127.2 156.3 %reduce-scatter.29.cloned.1.call-start = ((), (), s32[]{:S(2)}) async-start(), calls=%async_computation.21 | async-start | bytes 2654208 | tf_op jit(solution)/shard_map/reduce_scatter | solution.py:379
  1135.3 186.7 %reduce-scatter.25.cloned.1.call-start = ((), (), s32[]{:S(2)}) async-start(), calls=%async_computation.19 | async-start | bytes 884736 | tf_op jit(solution)/shard_map/reduce_scatter | solution.py:377
  1139.6 221.1 %reduce-scatter.31.cloned.1.call-start = ((), (), s32[]{:S(2)}) async-start(), calls=%async_computation.22 | async-start | bytes 884736
  1144.6 254.6 %reduce-scatter.33.cloned.1.call-start = ((), (), s32[]{:S(2)}) async-start(), calls=%async_computation.23 | async-start | bytes 884736
  1148.9 289.0 %reduce-scatter.35.cloned.1.call-start = ((), (), s32[]{:S(2)}) async-start(), calls=%async_computation.24 | async-start | bytes 884736
  1153.4 4.2 copy-start.24
  1153.4 4.6 copy-start.12
  1154.6 6.8 copy-start.20
  1154.6 6.8 copy-start.21
  1154.6 6.8 copy-start.22
  1154.6 6.8 copy-start.23
  1154.6 43.3 %copy-start.13 = (f32[640,768]{1,0:T(8,128)S(1)}, f32[640,768]{1,0:T(8,128)}, u32[]{:S(2)}) copy-start(f32[640,768]{1,0:T(8,128)} %get-tuple-element.363) | copy-start | bytes 5898244
Sparse Core Ops, SparseCore 0:
  10.4 79.1 all-gather.6
  184.2 134.8 reduce-scatter.16
  426.8 135.3 reduce-scatter.18
  568.1 76.9 all-gather.12
  662.2 134.7 reduce-scatter.20
  805.0 76.9 all-gather.14
  1119.2 71.1 reduce-scatter.22
  1194.3 42.7 reduce-scatter.26
  1241.1 42.3 reduce-scatter.28
  1287.0 34.9 reduce-scatter.24
  1325.7 34.9 reduce-scatter.30
  1364.3 34.9 reduce-scatter.32
  1403.0 34.9 reduce-scatter.34
Sparse Core Ops, SparseCore 1:
  186.5 22.3 all-gather.8
  371.0 24.4 all-gather.10
